TPU v7x, 128 devices: a whole 4x4x4 slice. The times are simulated.
128 devices in a mesh: dp: 64 (over z, y, x), tensor: 2 (over core).
Axes of the slice: x: 4, y: 4, z: 4, core: 2. Of those that a mesh axis runs over, the one named last changes fastest.
Arguments:
- tokens: bfloat16 [49152, 768], P(('dp', 'tensor')), may hold values from -6 to 6
- skip_tokens: bfloat16 [49152, 768], P(('dp', 'tensor')), may hold values from -6 to 6
- cot_back: bfloat16 [49152, 768], P(('dp', 'tensor')), may hold values from -6 to 6
- cot_head: bfloat16 [49152, 768], P(('dp', 'tensor')), may hold values from -6 to 6
- one_span: int32 [192], P('dp'), may hold values 0 or 1
- lower_qkv: bfloat16 [3, 768, 768], P(None, None, 'tensor'), may hold values from -0.21875 to 0.21875
- lower_proj: bfloat16 [768, 768], P('tensor'), may hold values from -1.75 to 1.75
- lower_gain_attn: float32 [768], replicated, may hold values from 0.1 to 1.9
- lower_shift_attn: float32 [768], replicated, may hold values from -1.5 to 1.5
- lower_w_in: bfloat16 [768, 3072], P(None, 'tensor'), may hold values from -0.21875 to 0.21875
- lower_w_out: bfloat16 [3072, 768], P('tensor'), may hold values from -0.15625 to 0.15625
- lower_gain_ffn: float32 [768], replicated, may hold values from 0.1 to 1.9
- lower_shift_ffn: float32 [768], replicated, may hold values from -1.5 to 1.5
- upper_qkv: bfloat16 [3, 768, 768], P(None, None, 'tensor'), may hold values from -0.21875 to 0.21875
- upper_proj: bfloat16 [768, 768], P('tensor'), may hold values from -1.75 to 1.75
- upper_gain_attn: float32 [768], replicated, may hold values from 0.1 to 1.9
- upper_shift_attn: float32 [768], replicated, may hold values from -1.5 to 1.5
- upper_w_in: bfloat16 [768, 3072], P(None, 'tensor'), may hold values from -0.21875 to 0.21875
- upper_w_out: bfloat16 [3072, 768], P('tensor'), may hold values from -0.15625 to 0.15625
- upper_gain_ffn: float32 [768], replicated, may hold values from 0.1 to 1.9
- upper_shift_ffn: float32 [768], replicated, may hold values from -1.5 to 1.5
Outputs:
- back_out: bfloat16 [49152, 768], P(('dp', 'tensor'))
- head_out: bfloat16 [49152, 768], P(('dp', 'tensor'))
- grad_tokens: float32 [49152, 768], P(('dp', 'tensor'))
- grad_skip: float32 [49152, 768], P(('dp', 'tensor'))
- grad_lower_qkv: float32 [3, 768, 768], P(None, None, 'tensor')
- grad_lower_proj: float32 [768, 768], P('tensor')
- grad_lower_gain_attn: float32 [768], replicated
- grad_lower_shift_attn: float32 [768], replicated
- grad_lower_w_in: float32 [768, 3072], P(None, 'tensor')
- grad_lower_w_out: float32 [3072, 768], P('tensor')
- grad_lower_gain_ffn: float32 [768], replicated
- grad_lower_shift_ffn: float32 [768], replicated
- grad_upper_qkv: float32 [3, 768, 768], P(None, None, 'tensor')
- grad_upper_proj: float32 [768, 768], P('tensor')
- grad_upper_gain_attn: float32 [768], replicated
- grad_upper_shift_attn: float32 [768], replicated
- grad_upper_w_in: float32 [768, 3072], P(None, 'tensor')
- grad_upper_w_out: float32 [3072, 768], P('tensor')
- grad_upper_gain_ffn: float32 [768], replicated
- grad_upper_shift_ffn: float32 [768], replicated
Inputs may be any that keep to these rules, and one draw needn't show every extreme that they name: `one_span`: 1 marks a document whose second span is padding: masked as keys, and zero in both outputs.
All inputs are finite; a program needn't handle non-finite values. No bound on the sum of `one_span` on one device may be relied on, other than what follows from the above.
Results may differ from a plain program's by a relative error of at most 0.02.
Values may be sent and summed in bfloat16 or wider, within the bound.
No kernel may reach another device: no remote copies, remote signals or barrier semaphores. Data moves between devices by JAX's collectives and lax.ppermute only.
A program may use at most 192 MiB of HBM per device.

v0:
```python
import jax
import jax.numpy as jnp
from jax import lax
from jax.sharding import PartitionSpec as P

HEAD_DIM = 64
SPAN = 128


EPS = 1e-06
SCALE = 0.125
NEG = -1000000000.0


def norm_forward(resid, gain, shift):
    mean = jnp.mean(resid, axis=-1, keepdims=True)
    centered = resid - mean
    var = jnp.mean(centered * centered, axis=-1, keepdims=True)
    inv_std = lax.rsqrt(var + EPS)
    normed = centered * inv_std
    return (normed * gain + shift, normed, inv_std)


def norm_backward(grad_out, normed, inv_std, gain):
    grad_normed = grad_out * gain
    first_mean = jnp.mean(grad_normed, axis=-1, keepdims=True)
    second_mean = jnp.mean(grad_normed * normed, axis=-1, keepdims=True)
    grad_resid = inv_std * (grad_normed - first_mean - normed * second_mean)
    return (grad_resid, jnp.sum(grad_out * normed, axis=0), jnp.sum(grad_out, axis=0))


def gelu_slope(value):
    return (
        0.5 * (1.0 + jax.scipy.special.erf(value * 0.7071067811865476))
        + value * jnp.exp(-0.5 * value * value) * 0.3989422804014327
    )


def contract_last(left, right):
    return lax.dot_general(
        left, right, (((1,), (1,)), ((), ())), preferred_element_type=jnp.float32
    )


def contract_rows(left, right):
    return lax.dot_general(
        left, right, (((0,), (0,)), ((), ())), preferred_element_type=jnp.float32
    )


def gather_rows(rows_low):
    return lax.all_gather(rows_low, "tensor", axis=0, tiled=True)


def gather_grad(rows_low):
    return lax.all_gather(rows_low, "tensor", axis=0, tiled=True)


def sum_rows(full, weight, count):

    def term(start, size):
        return jnp.dot(full, weight, preferred_element_type=jnp.float32)

    return lax.psum_scatter(
        term(jnp.int32(0), count * lax.axis_size("tensor")).astype(jnp.bfloat16),
        "tensor",
        scatter_dimension=0,
        tiled=True,
    ).astype(jnp.float32)


def sum_back(term, count):
    return lax.psum_scatter(
        term(jnp.int32(0), count * lax.axis_size("tensor")).astype(jnp.bfloat16),
        "tensor",
        scatter_dimension=0,
        tiled=True,
    ).astype(jnp.float32)


def split_heads(full_qkv, index, docs):
    rows, _, width = full_qkv.shape
    return full_qkv[:, index].reshape(docs, 2 * SPAN, width // HEAD_DIM, HEAD_DIM)


def attend(qkv, key_ok):
    docs = key_ok.shape[0]
    rows, _, width = qkv.shape
    query = split_heads(qkv, 0, docs).astype(jnp.bfloat16)
    keys = split_heads(qkv, 1, docs).astype(jnp.bfloat16)
    values = split_heads(qkv, 2, docs).astype(jnp.bfloat16)
    scores = jnp.einsum("nqhe,nkhe->nhqk", query, keys, preferred_element_type=jnp.float32) * SCALE
    scores = jnp.where(key_ok[:, None, None, :], scores, NEG)
    largest = jnp.max(scores, axis=-1, keepdims=True)
    raised = jnp.exp(scores - largest)
    total = jnp.sum(raised, axis=-1, keepdims=True)
    log_total = largest + jnp.log(total)
    prob_low = (raised / total).astype(jnp.bfloat16)
    mixed = jnp.einsum("nhqk,nkhe->nqhe", prob_low, values, preferred_element_type=jnp.float32)
    context = mixed.reshape(rows, width).astype(jnp.bfloat16)
    return (context, (query, keys, values, log_total))


def attend_back(grad_ctx, kept, key_ok):
    query, keys, values, log_total = kept
    docs, length, heads, size = query.shape
    scores = jnp.einsum("nqhe,nkhe->nhqk", query, keys, preferred_element_type=jnp.float32) * SCALE
    scores = jnp.where(key_ok[:, None, None, :], scores, NEG)
    prob = jnp.exp(scores - log_total)
    prob_low = prob.astype(jnp.bfloat16)
    grad_mix = grad_ctx.reshape(docs, length, heads, size)
    grad_values = jnp.einsum(
        "nhqk,nqhe->nkhe", prob_low, grad_mix, preferred_element_type=jnp.float32
    )
    grad_prob = jnp.einsum("nqhe,nkhe->nhqk", grad_mix, values, preferred_element_type=jnp.float32)
    grad_scores = prob * (grad_prob - jnp.sum(grad_prob * prob, axis=-1, keepdims=True))
    grad_scores = grad_scores.astype(jnp.bfloat16)
    grad_query = (
        jnp.einsum("nhqk,nkhe->nqhe", grad_scores, keys, preferred_element_type=jnp.float32) * SCALE
    )
    grad_keys = (
        jnp.einsum("nhqk,nqhe->nkhe", grad_scores, query, preferred_element_type=jnp.float32)
        * SCALE
    )
    rows = docs * length
    width = heads * size
    stacked = jnp.stack(
        [
            grad_query.reshape(rows, width),
            grad_keys.reshape(rows, width),
            grad_values.reshape(rows, width),
        ],
        axis=1,
    )
    return stacked.astype(jnp.bfloat16)


def block_forward(rows, weights, key_ok, count):
    qkv_w, proj_w, gain_a, shift_a, in_w, out_w, gain_f, shift_f = weights
    full = gather_rows(rows.astype(jnp.bfloat16))
    qkv = jnp.einsum("rd,cdj->rcj", full, qkv_w, preferred_element_type=jnp.float32)
    context, att_kept = attend(qkv, key_ok)
    attn = sum_rows(context, proj_w, count)
    first, normed_a, inv_a = norm_forward(rows + attn, gain_a, shift_a)
    full_first = gather_rows(first.astype(jnp.bfloat16))
    pre = jnp.dot(full_first, in_w, preferred_element_type=jnp.float32)
    act = jax.nn.gelu(pre, approximate=False).astype(jnp.bfloat16)
    ffn = sum_rows(act, out_w, count)
    result, normed_f, inv_f = norm_forward(first + ffn, gain_f, shift_f)
    return (
        result,
        (full, att_kept, context, normed_a, inv_a, full_first, pre, act, normed_f, inv_f),
    )


def block_backward(grad_out, weights, key_ok, count, kept):
    qkv_w, proj_w, gain_a, shift_a, in_w, out_w, gain_f, shift_f = weights
    full, att_kept, context, normed_a, inv_a, full_first, pre, act, normed_f, inv_f = kept
    grad_second, grad_gain_f, grad_shift_f = norm_backward(grad_out, normed_f, inv_f, gain_f)
    full_grad_ffn = gather_grad(grad_second.astype(jnp.bfloat16))
    grad_act = contract_last(full_grad_ffn, out_w)
    grad_out_w = contract_rows(act, full_grad_ffn)
    grad_pre = (grad_act * gelu_slope(pre)).astype(jnp.bfloat16)
    grad_in_w = contract_rows(full_first, grad_pre)

    def ffn_term(start, size):
        return contract_last(grad_pre, in_w)

    grad_first = grad_second + sum_back(ffn_term, count)
    grad_resid, grad_gain_a, grad_shift_a = norm_backward(grad_first, normed_a, inv_a, gain_a)
    full_grad_attn = gather_grad(grad_resid.astype(jnp.bfloat16))
    grad_ctx = contract_last(full_grad_attn, proj_w).astype(jnp.bfloat16)
    grad_proj = contract_rows(context, full_grad_attn)
    grad_qkv = attend_back(grad_ctx, att_kept, key_ok)
    grad_qkv_w = jnp.einsum("rd,rcj->cdj", full, grad_qkv, preferred_element_type=jnp.float32)

    def attn_term(start, size):
        return jnp.einsum("rcj,cdj->rd", grad_qkv, qkv_w, preferred_element_type=jnp.float32)

    grad_rows = grad_resid + sum_back(attn_term, count)
    return (
        grad_rows,
        (grad_qkv_w, grad_proj, grad_in_w, grad_out_w),
        (grad_gain_a, grad_shift_a, grad_gain_f, grad_shift_f),
    )


def on_device(
    tokens,
    skip_tokens,
    cot_back,
    cot_head,
    one_span,
    lower_qkv,
    lower_proj,
    lower_gain_attn,
    lower_shift_attn,
    lower_w_in,
    lower_w_out,
    lower_gain_ffn,
    lower_shift_ffn,
    upper_qkv,
    upper_proj,
    upper_gain_attn,
    upper_shift_attn,
    upper_w_in,
    upper_w_out,
    upper_gain_ffn,
    upper_shift_ffn,
):
    count = tokens.shape[0]
    docs_local = one_span.shape[0]
    position = jnp.arange(2 * SPAN)
    key_ok = (position[None, :] < SPAN) | (one_span[:, None] == 0)
    row_index = lax.axis_index("tensor") * count + jnp.arange(count)
    doc_index = row_index // (2 * SPAN)
    doc_flag = jnp.sum(
        jnp.where(doc_index[:, None] == jnp.arange(docs_local)[None, :], one_span[None, :], 0),
        axis=1,
    )
    row_ok = (row_index // SPAN % 2 == 0) | (doc_flag == 0)
    valid = row_ok[:, None].astype(jnp.float32)
    is_cls = (row_index % SPAN == 0)[:, None]
    lower = (
        lower_qkv,
        lower_proj,
        lower_gain_attn,
        lower_shift_attn,
        lower_w_in,
        lower_w_out,
        lower_gain_ffn,
        lower_shift_ffn,
    )
    upper = (
        upper_qkv,
        upper_proj,
        upper_gain_attn,
        upper_shift_attn,
        upper_w_in,
        upper_w_out,
        upper_gain_ffn,
        upper_shift_ffn,
    )
    back, kept_lower = block_forward(tokens.astype(jnp.float32), lower, key_ok, count)
    head_in = jnp.where(is_cls, back, skip_tokens.astype(jnp.float32))
    head, kept_upper = block_forward(head_in, upper, key_ok, count)
    head_again, kept_upper = block_forward(head_in, upper, key_ok, count)
    grad_head_in, weights_upper, norms_upper = block_backward(
        cot_head.astype(jnp.float32) * valid, upper, key_ok, count, kept_upper
    )
    grad_skip = jnp.where(is_cls, 0.0, grad_head_in)
    grad_back = cot_back.astype(jnp.float32) * valid + jnp.where(is_cls, grad_head_in, 0.0)
    back_again, kept_lower = block_forward(tokens.astype(jnp.float32), lower, key_ok, count)
    grad_tokens, weights_lower, norms_lower = block_backward(
        grad_back, lower, key_ok, count, kept_lower
    )
    summed = lax.psum(
        (
            weights_lower[0],
            weights_lower[1],
            weights_lower[2],
            weights_lower[3],
            weights_upper[0],
            weights_upper[1],
            weights_upper[2],
            weights_upper[3],
        ),
        "dp",
    )
    weights_lower = summed[:4]
    weights_upper = summed[4:]
    norms = lax.psum(
        (
            norms_lower[0],
            norms_lower[1],
            norms_lower[2],
            norms_lower[3],
            norms_upper[0],
            norms_upper[1],
            norms_upper[2],
            norms_upper[3],
        ),
        ("dp", "tensor"),
    )
    return (
        (back * valid).astype(jnp.bfloat16),
        (head * valid).astype(jnp.bfloat16),
        grad_tokens,
        grad_skip,
        weights_lower[0],
        weights_lower[1],
        norms[0],
        norms[1],
        weights_lower[2],
        weights_lower[3],
        norms[2],
        norms[3],
        weights_upper[0],
        weights_upper[1],
        norms[4],
        norms[5],
        weights_upper[2],
        weights_upper[3],
        norms[6],
        norms[7],
    )


def solution(mesh):
    return jax.shard_map(
        on_device,
        mesh=mesh,
        in_specs=(
            P(("dp", "tensor"), None),
            P(("dp", "tensor"), None),
            P(("dp", "tensor"), None),
            P(("dp", "tensor"), None),
            P("dp"),
            P(None, None, "tensor"),
            P("tensor", None),
            P(),
            P(),
            P(None, "tensor"),
            P("tensor", None),
            P(),
            P(),
            P(None, None, "tensor"),
            P("tensor", None),
            P(),
            P(),
            P(None, "tensor"),
            P("tensor", None),
            P(),
            P(),
        ),
        out_specs=(
            P(("dp", "tensor"), None),
            P(("dp", "tensor"), None),
            P(("dp", "tensor"), None),
            P(("dp", "tensor"), None),
            P(None, None, "tensor"),
            P("tensor", None),
            P(),
            P(),
            P(None, "tensor"),
            P("tensor", None),
            P(),
            P(),
            P(None, None, "tensor"),
            P("tensor", None),
            P(),
            P(),
            P(None, "tensor"),
            P("tensor", None),
            P(),
            P(),
        ),
        check_vma=False,
    )
```

profile of v0, /device:TPU:32, one launch (start us, length us, event | category | flops | bytes accessed | tf_op | source)
XLA Modules:
  0.0 767.2 jit_solution(13849110559285241744)
XLA Ops:
  8.7 15.0 %all-gather.9.cloned.1.call-done = bf16[768,768]{1,0:T(8,128)(2,1)} async-done(((bf16[384,768]{1,0:T(8,128)(2,1)}), bf16[768,768]{1,0:T(8,128)(2,1)}) %all-gather.9.cloned.1.call-update) | async-done | bytes 1179664 | tf_op jit(solution)/shard_map/all_gather | solution.py:52
  23.7 3.5 convolution_convert_fusion.1
  35.5 3.2 reshape.273
  48.9 12.8 %reduce-scatter.9.cloned.1.call-done = bf16[384,768]{1,0:T(8,128)(2,1)} async-done(((bf16[768,768]{1,0:T(8,128)(2,1)}), bf16[384,768]{1,0:T(8,128)(2,1)}) %reduce-scatter.9.cloned.1.call-update) | async-done | bytes 589840 | tf_op jit(solution)/shard_map/reduce_scatter | solution.py:64
  65.9 13.2 %all-gather.11.cloned.1.call-done = bf16[768,768]{1,0:T(8,128)(2,1)} async-done(((bf16[384,768]{1,0:T(8,128)(2,1)}), bf16[768,768]{1,0:T(8,128)(2,1)}) %all-gather.11.cloned.1.call-update) | async-done | bytes 1179664 | tf_op jit(solution)/shard_map/all_gather | solution.py:52
  79.1 14.4 %fusion.2 = (bf16[768,1536]{1,0:T(8,128)(2,1)S(1)}, f32[768,1536]{1,0:T(8,128)}) fusion(bf16[768,768]{1,0:T(8,128)(2,1)} %all-gather.11.cloned.1.call-done, bf16[768,1536]{1,0:T(8,128)(2,1)} %param.30), kind=kOutput, calls=%fused_computation.6 | convolution fusion | flops 1888616448 | bytes 10616832 | tf_op jit(solution)/shard_map/dot_general | solution.py:146
  94.9 3.0 convolution_convert_fusion.7
  98.5 12.3 %reduce-scatter.11.cloned.1.call-done = bf16[384,768]{1,0:T(8,128)(2,1)} async-done(((bf16[768,768]{1,0:T(8,128)(2,1)}), bf16[384,768]{1,0:T(8,128)(2,1)}) %reduce-scatter.11.cloned.1.call-update) | async-done | bytes 589840 | tf_op jit(solution)/shard_map/reduce_scatter | solution.py:64
  117.3 12.9 %all-gather.13.cloned.1.call-done = bf16[768,768]{1,0:T(8,128)(2,1)} async-done(((bf16[384,768]{1,0:T(8,128)(2,1)}), bf16[768,768]{1,0:T(8,128)(2,1)}) %all-gather.13.cloned.1.call-update) | async-done | bytes 1179664 | tf_op jit(solution)/shard_map/all_gather | solution.py:52
  130.2 3.5 convolution_convert_fusion
  135.0 3.0 reshape.278
  140.5 3.0 reshape.277
  146.0 3.0 reshape.276
  161.9 11.5 %reduce-scatter.13.cloned.1.call-done = bf16[384,768]{1,0:T(8,128)(2,1)} async-done(((bf16[768,768]{1,0:T(8,128)(2,1)}), bf16[384,768]{1,0:T(8,128)(2,1)}) %reduce-scatter.13.cloned.1.call-update) | async-done | bytes 589840 | tf_op jit(solution)/shard_map/reduce_scatter | solution.py:64
  173.4 2.8 fusion.99
  179.1 13.2 %all-gather.15.cloned.1.call-done = bf16[768,768]{1,0:T(8,128)(2,1)} async-done(((bf16[384,768]{1,0:T(8,128)(2,1)}), bf16[768,768]{1,0:T(8,128)(2,1)}) %all-gather.15.cloned.1.call-update) | async-done | bytes 1179664 | tf_op jit(solution)/shard_map/all_gather | solution.py:52
  192.3 13.7 %fusion.5 = (bf16[768,1536]{1,0:T(8,128)(2,1)S(1)}, f32[768,1536]{1,0:T(8,128)}) fusion(bf16[768,768]{1,0:T(8,128)(2,1)} %all-gather.15.cloned.1.call-done, bf16[768,1536]{1,0:T(8,128)(2,1)S(1)} %copy-done), kind=kOutput, calls=%fused_computation.9 | convolution fusion | flops 1888616448 | bytes 10616832 | tf_op jit(solution)/shard_map/dot_general | solution.py:146
  207.4 3.0 convolution_convert_fusion.6
  210.5 12.8 %reduce-scatter.15.cloned.1.call-done = bf16[384,768]{1,0:T(8,128)(2,1)} async-done(((bf16[768,768]{1,0:T(8,128)(2,1)}), bf16[384,768]{1,0:T(8,128)(2,1)}) %reduce-scatter.15.cloned.1.call-update) | async-done | bytes 589840 | tf_op jit(solution)/shard_map/reduce_scatter | solution.py:64
  230.4 13.3 %all-gather.17.cloned.1.call-done = bf16[768,768]{1,0:T(8,128)(2,1)} async-done(((bf16[384,768]{1,0:T(8,128)(2,1)}), bf16[768,768]{1,0:T(8,128)(2,1)}) %all-gather.17.cloned.1.call-update) | async-done | bytes 1179664 | tf_op jit(solution)/shard_map/all_gather | solution.py:56
  243.8 5.4 fusion.11
  250.6 3.0 convolution_convert_fusion.5
  253.7 12.8 %reduce-scatter.17.cloned.1.call-done = bf16[384,768]{1,0:T(8,128)(2,1)} async-done(((bf16[768,768]{1,0:T(8,128)(2,1)}), bf16[384,768]{1,0:T(8,128)(2,1)}) %reduce-scatter.17.cloned.1.call-update) | async-done | bytes 589840 | tf_op jit(solution)/shard_map/reduce_scatter | solution.py:73
  266.5 3.1 multiply_reduce_fusion.3
  273.0 12.4 %all-gather.19.cloned.1.call-done = bf16[768,768]{1,0:T(8,128)(2,1)} async-done(((bf16[384,768]{1,0:T(8,128)(2,1)}), bf16[768,768]{1,0:T(8,128)(2,1)}) %all-gather.19.cloned.1.call-update) | async-done | bytes 1179664 | tf_op jit(solution)/shard_map/all_gather | solution.py:56
  289.4 4.2 fusion.65
  293.5 3.5 multiply_reduce_fusion.1
  314.7 2.7 bitcast_convert_fusion.1
  317.5 12.8 %reduce-scatter.19.cloned.1.call-done = bf16[384,768]{1,0:T(8,128)(2,1)} async-done(((bf16[768,768]{1,0:T(8,128)(2,1)}), bf16[384,768]{1,0:T(8,128)(2,1)}) %reduce-scatter.19.cloned.1.call-update) | async-done | bytes 589840 | tf_op jit(solution)/shard_map/reduce_scatter | solution.py:73
  330.3 3.5 multiply_reduce_fusion.4
  335.5 12.9 %all-gather.21.cloned.1.call-done = bf16[768,768]{1,0:T(8,128)(2,1)} async-done(((bf16[384,768]{1,0:T(8,128)(2,1)}), bf16[768,768]{1,0:T(8,128)(2,1)}) %all-gather.21.cloned.1.call-update) | async-done | bytes 1179664 | tf_op jit(solution)/shard_map/all_gather | solution.py:56
  348.4 5.5 fusion.17
  355.4 3.0 convolution_convert_fusion.4
  358.5 12.8 %reduce-scatter.21.cloned.1.call-done = bf16[384,768]{1,0:T(8,128)(2,1)} async-done(((bf16[768,768]{1,0:T(8,128)(2,1)}), bf16[384,768]{1,0:T(8,128)(2,1)}) %reduce-scatter.21.cloned.1.call-update) | async-done | bytes 589840 | tf_op jit(solution)/shard_map/reduce_scatter | solution.py:73
  375.6 6.4 fusion.109
  382.0 4.2 fusion.108
  392.9 4.2 fusion.62
  397.1 3.5 multiply_reduce_fusion
  412.9 2.7 bitcast_convert_fusion
  417.6 5.0 convolution_bitcast_fusion
  422.6 4.3 fusion.106
  426.9 4.2 fusion.105
  433.4 3.4 convolution_bitcast_fusion.1
  437.6 69.7 %all-reduce = (f32[768]{0:T(1024)}, f32[768]{0:T(1024)}, f32[768]{0:T(1024)}, f32[768]{0:T(1024)}, f32[768]{0:T(1024)}, /*index=5*/f32[768]{0:T(1024)}, f32[768]{0:T(1024)}, f32[768]{0:T(1024)}) all-reduce(f32[768]{0:T(1024)S(1)} %get-tuple-element.82, f32[768]{0:T(1024)S(1)} %copy-done.68, ...), channel_id=1, replica_groups=mesh['dp'=64,'tensor'=2] {'dp','tensor'}, use_global_device_ids=true, to_apply=%region_34.35 | all-reduce | flops 6144 | bytes 49152 | tf_op jit(solution)/shard_map/psum | solution.py:272
  509.4 223.9 %all-reduce.4.cloned.1.call-done = (f32[3,768,384]{1,2,0:T(8,128)}, f32[384,768]{1,0:T(8,128)}, f32[768,1536]{1,0:T(8,128)}, f32[1536,768]{1,0:T(8,128)}, f32[3,...) async-done(((f32[3,768,384]{1,2,0:T(8,128)}, f32[384,768]{1,0:T(8,128)}, f32[768,1536]{1,0:T(8,128)}, f32[1536,768]{1,0:T(8,128)}, ...) | async-done | bytes 28311568 | tf_op jit(solution)/shard_map/psum | solution.py:257
  733.3 5.2 copy.167
  738.5 5.3 copy.168
  744.8 5.5 copy.222
  (337 shorter events, 133.5 us)
Async XLA Ops:
  7.2 185.1 %copy-start = (bf16[768,1536]{1,0:T(8,128)(2,1)S(1)}, bf16[768,1536]{1,0:T(8,128)(2,1)}, u32[]{:S(2)}) copy-start(bf16[768,1536]{1,0:T(8,128)(2,1)} %param.38) | copy-start | bytes 7077892
  7.2 16.5 %all-gather.9.cloned.1.call-start = ((), (), s32[]{:S(2)}) async-start(), calls=%async_computation.8 | async-start | bytes 1769472 | tf_op jit(solution)/shard_map/all_gather | solution.py:52
  7.9 53.8 %reduce-scatter.9.cloned.1.call-start = ((), (), s32[]{:S(2)}) async-start(), calls=%async_computation.9 | async-start | bytes 1769472 | tf_op jit(solution)/shard_map/reduce_scatter | solution.py:64
  8.7 32.5 %copy-start.71 = (pred[3,256]{1,0:T(4,128)(4,1)}, pred[3,256]{1,0:T(4,128)(4,1)S(1)}, u32[]{:S(2)}) copy-start(pred[3,256]{1,0:T(4,128)(4,1)S(1)} %broadcast_or_fusion) | copy-start | bytes 2308
  31.9 9.4 %copy-start.10 = (bf16[3,256,6,64]{1,3,2,0:T(8,128)(2,1)}, bf16[3,256,6,64]{1,3,2,0:T(8,128)(2,1)S(1)}, u32[]{:S(2)}) copy-start(bf16[3,256,6,64]{1,3,2,0:T(8,128)(2,1)S(1)} %copy.123) | copy-start | bytes 1769476
  35.5 6.9 copy-start.13
  46.1 15.7 %copy-start.4 = (bf16[384,768]{1,0:T(8,128)(2,1)S(1)}, bf16[384,768]{1,0:T(8,128)(2,1)}, u32[]{:S(2)}) copy-start(bf16[384,768]{1,0:T(8,128)(2,1)} %param.21) | copy-start | bytes 1769476
  48.8 15.7 %copy-start.52 = (f32[768]{0:T(1024)S(1)}, f32[768]{0:T(1024)}, u32[]{:S(2)}) copy-start(f32[768]{0:T(1024)} %param.28) | copy-start | bytes 9220
  48.8 15.7 %copy-start.56 = (f32[768]{0:T(1024)S(1)}, f32[768]{0:T(1024)}, u32[]{:S(2)}) copy-start(f32[768]{0:T(1024)} %param.29) | copy-start | bytes 9220
  48.8 30.3 %all-gather.11.cloned.1.call-start = ((), (), s32[]{:S(2)}) async-start(), calls=%async_computation.10 | async-start | bytes 1769472 | tf_op jit(solution)/shard_map/all_gather | solution.py:52
  65.7 45.2 %reduce-scatter.11.cloned.1.call-start = ((), (), s32[]{:S(2)}) async-start(), calls=%async_computation.11 | async-start | bytes 1769472 | tf_op jit(solution)/shard_map/reduce_scatter | solution.py:64
  79.1 15.8 %copy-start.75 = (bf16[1536,768]{1,0:T(8,128)(2,1)S(1)}, bf16[1536,768]{1,0:T(8,128)(2,1)}, u32[]{:S(2)}) copy-start(bf16[1536,768]{1,0:T(8,128)(2,1)} %param.31) | copy-start | bytes 7077892
  97.9 32.3 %all-gather.13.cloned.1.call-start = ((), (), s32[]{:S(2)}) async-start(), calls=%async_computation.12 | async-start | bytes 1769472 | tf_op jit(solution)/shard_map/all_gather | solution.py:52
  116.8 56.5 %reduce-scatter.13.cloned.1.call-start = ((), (), s32[]{:S(2)}) async-start(), calls=%async_computation.13 | async-start | bytes 1769472 | tf_op jit(solution)/shard_map/reduce_scatter | solution.py:64
  146.0 5.5 copy-start.72
  157.6 15.7 %copy-start.58 = (f32[768]{0:T(1024)S(1)}, f32[768]{0:T(1024)}, u32[]{:S(2)}) copy-start(f32[768]{0:T(1024)} %param.32) | copy-start | bytes 9220
  160.5 31.8 %all-gather.15.cloned.1.call-start = ((), (), s32[]{:S(2)}) async-start(), calls=%async_computation.14 | async-start | bytes 1769472 | tf_op jit(solution)/shard_map/all_gather | solution.py:52
  173.4 4.4 copy-start.63
  178.9 44.5 %reduce-scatter.15.cloned.1.call-start = ((), (), s32[]{:S(2)}) async-start(), calls=%async_computation.15 | async-start | bytes 1769472 | tf_op jit(solution)/shard_map/reduce_scatter | solution.py:64
  192.3 15.1 %copy-start.74 = (bf16[1536,768]{1,0:T(8,128)(2,1)S(1)}, bf16[1536,768]{1,0:T(8,128)(2,1)}, u32[]{:S(2)}) copy-start(bf16[1536,768]{1,0:T(8,128)(2,1)} %param.39) | copy-start | bytes 7077892
  210.5 33.3 %all-gather.17.cloned.1.call-start = ((), (), s32[]{:S(2)}) async-start(), calls=%async_computation.16 | async-start | bytes 1769472 | tf_op jit(solution)/shard_map/all_gather | solution.py:56
  230.4 36.1 %reduce-scatter.17.cloned.1.call-start = ((), (), s32[]{:S(2)}) async-start(), calls=%async_computation.17 | async-start | bytes 1769472 | tf_op jit(solution)/shard_map/reduce_scatter | solution.py:73
  253.6 16.0 %copy-start.6 = (f32[384,768]{1,0:T(8,128)S(1)}, f32[384,768]{1,0:T(8,128)}, u32[]{:S(2)}) copy-start(f32[384,768]{1,0:T(8,128)} %copy-done.5) | copy-start | bytes 3538948
  253.6 16.0 %copy-start.9 = (f32[384,768]{1,0:T(8,128)S(1)}, f32[384,768]{1,0:T(8,128)}, u32[]{:S(2)}) copy-start(f32[384,768]{1,0:T(8,128)} %get-tuple-element.120) | copy-start | bytes 3538948
  253.6 31.8 %all-gather.19.cloned.1.call-start = ((), (), s32[]{:S(2)}) async-start(), calls=%async_computation.18 | async-start | bytes 1769472 | tf_op jit(solution)/shard_map/all_gather | solution.py:56
  272.0 58.3 %reduce-scatter.19.cloned.1.call-start = ((), (), s32[]{:S(2)}) async-start(), calls=%async_computation.19 | async-start | bytes 1769472 | tf_op jit(solution)/shard_map/reduce_scatter | solution.py:73
  273.0 20.5 %copy-start.45 = (f32[3,6,256]{2,1,0:T(8,128)}, f32[3,6,256]{2,1,0:T(8,128)S(1)}, u32[]{:S(2)}) copy-start(f32[3,6,256]{2,1,0:T(8,128)S(1)} %log_add_fusion.1) | copy-start | bytes 55300
  289.4 7.7 %slice-start.2 = ((s8[4718592]{0:T(1024)(128)(4,1)}), s8[4194304]{0:T(1024)(128)(4,1)S(1)}, s32[]{:S(2)}) async-start(s8[4718592]{0:T(1024)(128)(4,1)} %bitcast.122), calls=%async_computation.27 | async-start | bytes 8388608
  314.6 15.7 %copy-start.8 = (f32[384,768]{1,0:T(8,128)S(1)}, f32[384,768]{1,0:T(8,128)}, u32[]{:S(2)}) copy-start(f32[384,768]{1,0:T(8,128)} %get-tuple-element.126) | copy-start | bytes 3538948
  314.6 15.7 %copy-start.18 = (f32[384,768]{1,0:T(8,128)S(1)}, f32[384,768]{1,0:T(8,128)}, u32[]{:S(2)}) copy-start(f32[384,768]{1,0:T(8,128)} %get-tuple-element.118) | copy-start | bytes 3538948
  314.6 15.7 %copy-start.59 = (f32[768]{0:T(1024)S(1)}, f32[768]{0:T(1024)}, u32[]{:S(2)}) copy-start(f32[768]{0:T(1024)} %param.32) | copy-start | bytes 9220
  317.4 31.0 %all-gather.21.cloned.1.call-start = ((), (), s32[]{:S(2)}) async-start(), calls=%async_computation.20 | async-start | bytes 1769472 | tf_op jit(solution)/shard_map/all_gather | solution.py:56
  335.0 36.3 %reduce-scatter.21.cloned.1.call-start = ((), (), s32[]{:S(2)}) async-start(), calls=%async_computation.21 | async-start | bytes 1769472 | tf_op jit(solution)/shard_map/reduce_scatter | solution.py:73
  348.4 6.9 copy-start.76
  358.4 30.5 %all-gather.23.cloned.1.call-start = ((), (), s32[]{:S(2)}) async-start(), calls=%async_computation.22 | async-start | bytes 1769472 | tf_op jit(solution)/shard_map/all_gather | solution.py:56
  375.5 131.8 %reduce-scatter.23.cloned.1.call-start = ((), (), s32[]{:S(2)}) async-start(), calls=%async_computation.23 | async-start | bytes 1769472 | tf_op jit(solution)/shard_map/reduce_scatter | solution.py:73
  375.6 6.4 copy-start.26
  375.6 6.4 copy-start.42
  382.0 6.9 copy-start.84
  392.9 7.7 %slice-start = ((s8[4718592]{0:T(1024)(128)(4,1)}), s8[4194304]{0:T(1024)(128)(4,1)S(1)}, s32[]{:S(2)}) async-start(s8[4718592]{0:T(1024)(128)(4,1)} %bitcast.120), calls=%async_computation.25 | async-start | bytes 8388608
  415.7 317.7 %all-reduce.4.cloned.1.call-start = ((), (), s32[]{:S(2)}) async-start(), calls=%async_computation.24 | async-start | bytes 56623104 | tf_op jit(solution)/shard_map/psum | solution.py:257
  417.6 5.0 copy-start.81
  417.6 5.0 copy-start.86
  436.8 70.4 %copy-start.17 = (f32[384,768]{1,0:T(8,128)S(1)}, f32[384,768]{1,0:T(8,128)}, u32[]{:S(2)}) copy-start(f32[384,768]{1,0:T(8,128)} %get-tuple-element.113) | copy-start | bytes 3538948
  738.5 5.3 copy-start.40
  738.5 11.8 %slice-start.8 = ((s8[4718592]{0:T(1024)(128)(4,1)}), s8[524288]{0:T(1024)(128)(4,1)S(1)}, s32[]{:S(2)}) async-start(s8[4718592]{0:T(1024)(128)(4,1)} %bitcast.128), calls=%async_computation.33 | async-start | bytes 1048576
  743.8 6.5 slice-start.9
  744.8 8.8 %slice-start.6 = ((s8[4718592]{0:T(1024)(128)(4,1)}), s8[4194304]{0:T(1024)(128)(4,1)S(1)}, s32[]{:S(2)}) async-start(s8[4718592]{0:T(1024)(128)(4,1)} %bitcast.126), calls=%async_computation.31 | async-start | bytes 8388608
  (67 other events, 153.9 us)
Sparse Core Ops, SparseCore 0:
  9.7 14.0 all-gather.8
  49.0 12.6 reduce-scatter.8
  65.8 13.2 all-gather.10
  98.1 12.7 reduce-scatter.10
  117.0 13.2 all-gather.12
  160.6 12.7 reduce-scatter.12
  179.0 13.2 all-gather.14
  210.6 12.7 reduce-scatter.14
  230.5 13.2 all-gather.16
  253.7 12.7 reduce-scatter.16
  272.1 13.2 all-gather.18
  317.5 12.7 reduce-scatter.18
  335.2 13.2 all-gather.20
  358.6 12.6 reduce-scatter.20
  375.6 13.2 all-gather.22
  415.8 12.6 reduce-scatter.22
  437.0 296.2 all-reduce.3
where the time goes:
time: 777 us; the launch traced here: 767 us
  waiting for transfers between devices  408 us (53%)
  matrix products  128 us (16%)
  local copies, waits for them, and re-layouts  98.1 us (13%)
  blocking collectives  69.7 us (9%)
  other arithmetic  45.2 us (6%)
  between operations  15.2 us (2%)
    psum x1, waiting for transfers between devices, on_device(): lax.psum((weights_lower[0], weights_lower[1], weights_lower[2], weights_l...  224 us
    psum x1, blocking collectives, on_device(): lax.psum((norms_lower[0], norms_lower[1], norms_lower[2], norms_lower[3],...  69.7 us
    all_gather x4, waiting for transfers between devices, gather_rows(): return lax.all_gather(rows_low, 'tensor', axis=0, tiled=True)  54.3 us
    reduce_scatter x4, waiting for transfers between devices, sum_rows(): lax.psum_scatter(term(jnp.int32(0), count * lax.axis_size('tensor')).asty...  49.4 us
    unnamed x210, local copies, waits for them, and re-layouts  46 us
    all_gather x4, waiting for transfers between devices, gather_grad(): return lax.all_gather(rows_low, 'tensor', axis=0, tiled=True)  41.4 us
    reduce_scatter x4, waiting for transfers between devices, sum_back(): lax.psum_scatter(term(jnp.int32(0), count * lax.axis_size('tensor')).asty...  38.5 us
    dot_general x2, matrix products, block_forward(): pre = jnp.dot(full_first, in_w, preferred_element_type=jnp.float32)  28.1 us
  transfers between devices with their start and end apart: 17, of which 16 were waited for; matrix products, arithmetic and copies ran while one was open for 5% of the time, Pallas kernels for 0%

commit v1 on v0

--- a/solution.py
+++ b/solution.py
@@ -48,12 +48,127 @@
     )
 
 
+SWAP = [(0, 1), (1, 0)]
+
+
 def gather_rows(rows_low):
-    return lax.all_gather(rows_low, "tensor", axis=0, tiled=True)
+    other = lax.ppermute(rows_low, "tensor", SWAP)
+    first = lax.axis_index("tensor") == 0
+    return jnp.concatenate(
+        [jnp.where(first, rows_low, other), jnp.where(first, other, rows_low)], axis=0
+    )
 
 
 def gather_grad(rows_low):
-    return lax.all_gather(rows_low, "tensor", axis=0, tiled=True)
+    return gather_rows(rows_low)
+
+
+def scatter_sum(full):
+    count = full.shape[0] // 2
+    side = lax.axis_index("tensor")
+    away = lax.dynamic_slice_in_dim(full, (1 - side) * count, count, 0).astype(jnp.bfloat16)
+    keep = lax.dynamic_slice_in_dim(full, side * count, count, 0)
+    return keep + lax.ppermute(away, "tensor", SWAP).astype(jnp.float32)
+
+
+BLOCK = (48, 384)
+
+
+def coord_bits(chip):
+    x, y, z = chip % 4, chip // 4 % 4, chip // 16
+    low = [(p ^ (p >> 1)) & 1 for p in (x, y, z)]
+    high = [p >> 1 for p in (x, y, z)]
+    return low, high
+
+
+def flip(chip, core, stage, mask):
+    pos = [chip % 4, chip // 4 % 4, chip // 16]
+    for axis in range(3):
+        if mask >> axis & 1:
+            low = (core == 0) == (stage == 0)
+            pos[axis] = pos[axis] ^ 1 if low else 3 - pos[axis]
+    return pos[0] + 4 * pos[1] + 16 * pos[2]
+
+
+def exchange(value, stage, mask):
+    pairs = [
+        (2 * chip + core, 2 * flip(chip, core, stage, mask) + core)
+        for chip in range(64)
+        for core in range(2)
+    ]
+    return lax.ppermute(value, ("dp", "tensor"), pairs)
+
+
+def my_bits():
+    low, high = coord_bits(lax.axis_index("dp"))
+    core = lax.axis_index("tensor")
+    first = [jnp.where(core == 0, a, b) for a, b in zip(low, high)]
+    second = [jnp.where(core == 0, b, a) for a, b in zip(low, high)]
+    near = first[0] + 2 * first[1] + 4 * first[2]
+    far = second[0] + 2 * second[1] + 4 * second[2]
+    return near, far
+
+
+def total(terms):
+    out = terms[0].astype(jnp.float32)
+    for term in terms[1:]:
+        out = out + term.astype(jnp.float32)
+    return out
+
+
+def sum_over_chips(blocks, turn, order):
+    rel = jnp.take(blocks, order, axis=0).reshape((2, 2, 2, 8) + BLOCK)
+    axes = [2 - (turn + j) % 3 for j in range(3)]
+    terms = [rel]
+    for axis in axes:
+        send = total([lax.slice_in_dim(t, 1, 2, axis=axis) for t in terms]).astype(jnp.bfloat16)
+        terms = [lax.slice_in_dim(t, 0, 1, axis=axis) for t in terms]
+        terms.append(exchange(send, 0, 1 << (2 - axis)))
+    terms = [t.reshape((8,) + BLOCK) for t in terms]
+    own = [total([t[0] for t in terms])]
+    for mask in range(1, 8):
+        own.append(exchange(total([t[mask] for t in terms]).astype(jnp.bfloat16), 1, mask))
+    mine = total(own).astype(jnp.bfloat16)
+    parts = [mine] + [exchange(mine, 1, mask) for mask in range(1, 8)]
+    held = jnp.stack(parts).reshape((1, 1, 1, 8) + BLOCK)
+    for axis in reversed(axes):
+        held = jnp.concatenate([held, exchange(held, 0, 1 << (2 - axis))], axis=axis)
+    return jnp.take(held.reshape((64,) + BLOCK), order, axis=0)
+
+
+def to_blocks(grad):
+    rows, columns = grad.shape
+    out = grad.astype(jnp.bfloat16).reshape(rows // 48, 48, columns // 384, 384)
+    return out.transpose(0, 2, 1, 3).reshape((-1,) + BLOCK)
+
+
+def from_blocks(blocks, shape):
+    rows, columns = shape
+    out = blocks.reshape(rows // 48, columns // 384, 48, 384).transpose(0, 2, 1, 3)
+    return out.reshape(shape).astype(jnp.float32)
+
+
+def sum_weights(grads, order):
+    qkv, proj, w_in, w_out = grads
+    attn = jnp.concatenate([to_blocks(qkv.reshape(-1, qkv.shape[-1])), to_blocks(proj)])
+    sum_out = sum_over_chips(to_blocks(w_out), 0, order)
+    sum_in = sum_over_chips(to_blocks(w_in), 1, order)
+    sum_attn = sum_over_chips(attn, 2, order)
+    return (
+        from_blocks(sum_attn[:48], (qkv.shape[0] * qkv.shape[1], qkv.shape[2])).reshape(qkv.shape),
+        from_blocks(sum_attn[48:], proj.shape),
+        from_blocks(sum_in, w_in.shape),
+        from_blocks(sum_out, w_out.shape),
+    )
+
+
+def sum_norms(norms):
+    value = jnp.stack(norms)
+    value = value + lax.ppermute(value, "tensor", SWAP)
+    for stage in range(2):
+        for axis in range(3):
+            value = value + exchange(value, stage, 1 << axis)
+    return [value[i] for i in range(8)]
 
 
 def sum_rows(full, weight, count):
@@ -61,21 +176,11 @@
     def term(start, size):
         return jnp.dot(full, weight, preferred_element_type=jnp.float32)
 
-    return lax.psum_scatter(
-        term(jnp.int32(0), count * lax.axis_size("tensor")).astype(jnp.bfloat16),
-        "tensor",
-        scatter_dimension=0,
-        tiled=True,
-    ).astype(jnp.float32)
+    return scatter_sum(term(jnp.int32(0), count * lax.axis_size("tensor")))
 
 
 def sum_back(term, count):
-    return lax.psum_scatter(
-        term(jnp.int32(0), count * lax.axis_size("tensor")).astype(jnp.bfloat16),
-        "tensor",
-        scatter_dimension=0,
-        tiled=True,
-    ).astype(jnp.float32)
+    return scatter_sum(term(jnp.int32(0), count * lax.axis_size("tensor")))
 
 
 def split_heads(full_qkv, index, docs):
@@ -244,44 +349,20 @@
     back, kept_lower = block_forward(tokens.astype(jnp.float32), lower, key_ok, count)
     head_in = jnp.where(is_cls, back, skip_tokens.astype(jnp.float32))
     head, kept_upper = block_forward(head_in, upper, key_ok, count)
-    head_again, kept_upper = block_forward(head_in, upper, key_ok, count)
     grad_head_in, weights_upper, norms_upper = block_backward(
         cot_head.astype(jnp.float32) * valid, upper, key_ok, count, kept_upper
     )
     grad_skip = jnp.where(is_cls, 0.0, grad_head_in)
     grad_back = cot_back.astype(jnp.float32) * valid + jnp.where(is_cls, grad_head_in, 0.0)
-    back_again, kept_lower = block_forward(tokens.astype(jnp.float32), lower, key_ok, count)
     grad_tokens, weights_lower, norms_lower = block_backward(
         grad_back, lower, key_ok, count, kept_lower
     )
-    summed = lax.psum(
-        (
-            weights_lower[0],
-            weights_lower[1],
-            weights_lower[2],
-            weights_lower[3],
-            weights_upper[0],
-            weights_upper[1],
-            weights_upper[2],
-            weights_upper[3],
-        ),
-        "dp",
-    )
-    weights_lower = summed[:4]
-    weights_upper = summed[4:]
-    norms = lax.psum(
-        (
-            norms_lower[0],
-            norms_lower[1],
-            norms_lower[2],
-            norms_lower[3],
-            norms_upper[0],
-            norms_upper[1],
-            norms_upper[2],
-            norms_upper[3],
-        ),
-        ("dp", "tensor"),
-    )
+    near, far = my_bits()
+    slots = jnp.arange(64)
+    order = (slots // 8 ^ near) * 8 + (slots % 8 ^ far)
+    weights_upper = sum_weights(weights_upper, order)
+    weights_lower = sum_weights(weights_lower, order)
+    norms = sum_norms(norms_lower + norms_upper)
     return (
         (back * valid).astype(jnp.bfloat16),
         (head * valid).astype(jnp.bfloat16),

time: 777 us -> 813 us (1.046)
  starting transfers between devices: 2.32 us -> 261 us
  waiting for transfers between devices: 408 us -> 153 us
  local copies, waits for them, and re-layouts: 98.1 us -> 177 us
  blocking collectives: 69.7 us -> 0 us
  other arithmetic: 45.2 us -> 108 us
  matrix products: 128 us -> 99.5 us
  between operations: 15.2 us -> 4.15 us
    ppermute x0 -> x143, starting transfers between devices: none -> 261 us  [the longest x126 248 us: exchange(): return lax.ppermute(value, ('dp', 'tensor'), pairs)]
    psum x1 -> x0, waiting for transfers between devices: 224 us -> none  [on_device(): lax.psum((weights_lower[0], weights_lower[1], weights_lower[2], weights_l...]
    ppermute x0 -> x143, waiting for transfers between devices: none -> 153 us  [the longest x126 134 us: exchange(): return lax.ppermute(value, ('dp', 'tensor'), pairs)]
    all_gather x8 -> x0, waiting for transfers between devices: 95.7 us -> none  [the longest x4 54.3 us: gather_rows(): return lax.all_gather(rows_low, 'tensor', axis=0, tiled=True)]
    reduce_scatter x8 -> x0, waiting for transfers between devices: 87.9 us -> none  [the longest x4 49.4 us: sum_rows(): lax.psum_scatter(term(jnp.int32(0), count * lax.axis_size('tensor')).asty...]
    psum x1 -> x0, blocking collectives: 69.7 us -> none  [on_device(): lax.psum((norms_lower[0], norms_lower[1], norms_lower[2], norms_lower[3],...]
    gather x0 -> x12, local copies, waits for them, and re-layouts: none -> 34.9 us  [the longest x6 21.2 us: sum_over_chips(): rel = jnp.take(blocks, order, axis=0).reshape((2, 2, 2, 8) + BLOCK)]
    reshape x0 -> x12, local copies, waits for them, and re-layouts: none -> 33.9 us  [to_blocks(): out = grad.astype(jnp.bfloat16).reshape(rows // 48, 48, columns // 384, 384)]
  transfers between devices with their start and end apart: 17 -> 143, of which waited for: 16 -> 42; matrix products, arithmetic and copies ran while one was open for 5% -> 22% of each run, Pallas kernels for 0% -> 0%
where the time goes in v1:
time: 813 us; the launch traced here: 803 us
  starting transfers between devices  261 us (32%)
  local copies, waits for them, and re-layouts  177 us (22%)
  waiting for transfers between devices  153 us (19%)
  other arithmetic  108 us (13%)
  matrix products  99.5 us (12%)
    ppermute x126, starting transfers between devices, exchange(): return lax.ppermute(value, ('dp', 'tensor'), pairs)  248 us
    ppermute x126, waiting for transfers between devices, exchange(): return lax.ppermute(value, ('dp', 'tensor'), pairs)  134 us
    reshape x12, local copies, waits for them, and re-layouts, to_blocks(): out = grad.astype(jnp.bfloat16).reshape(rows // 48, 48, columns // 384, 384)  33.9 us
    unnamed x432, local copies, waits for them, and re-layouts  33.8 us
    dot_general x2, matrix products, block_forward(): pre = jnp.dot(full_first, in_w, preferred_element_type=jnp.float32)  24.3 us
    gather x6, local copies, waits for them, and re-layouts, sum_over_chips(): rel = jnp.take(blocks, order, axis=0).reshape((2, 2, 2, 8) + BLOCK)  21.2 us
    concatenate x18, other arithmetic, sum_over_chips(): held = jnp.concatenate([held, exchange(held, 0, 1 << 2 - axis)], axis=axis)  18.5 us
  transfers between devices with their start and end apart: 143, of which 42 were waited for; matrix products, arithmetic and copies ran while one was open for 22% of the time, Pallas kernels for 0%

profile of v1, /device:TPU:32, one launch (start us, length us, event | category | flops | bytes accessed | tf_op | source)
XLA Modules:
  0.0 803.1 jit_solution(9396015617005252332)
XLA Ops:
  35.4 13.1 %fusion.2 = (bf16[768,1536]{1,0:T(8,128)(2,1)S(1)}, f32[768,1536]{1,0:T(8,128)}) fusion(bf16[768,1536]{1,0:T(8,128)(2,1)S(1)} %copy-done.175, bf16[384,768]{1,0:T(8,128)(2,1)S(1)} %get-tuple-element.142, bf16[384,768]{1,0:T(8,128)(2,1)S(1)} %get-tuple-element.141), kind=kOutput, calls=%fused_computation.18 | convolution fusion | flops 1890975744 | bytes 10616832 | tf_op jit(solution)/shard_map/dot_general | solution.py:251
  82.4 9.0 %collective-permute-start.6 = (bf16[384,768]{1,0:T(8,128)(2,1)S(1)}, bf16[384,768]{1,0:T(8,128)(2,1)S(1)}, u32[]{:S(2)}, u32[]{:S(2)}) collective-permute-start(bf16[384,768]{1,0:T(8,128)(2,1)S(1)} %fusion.72), channel_id=1, source_target_pairs={{0,1},{1,0},{2,3},{3,2},{4,5},{5,4},{6,7},{7,6},{8,9},{9,8},{10,11... | collective-permute-start | bytes 1769480 | tf_op jit(solution)/shard_map/ppermute | solution.py:55
  93.7 11.2 %fusion.5 = (bf16[768,1536]{1,0:T(8,128)(2,1)S(1)}, f32[768,1536]{1,0:T(8,128)S(1)}) fusion(bf16[768,1536]{1,0:T(8,128)(2,1)S(1)} %copy-done, bf16[384,768]{1,0:T(8,128)(2,1)S(1)} %get-tuple-element.138, bf16[384,768]{1,0:T(8,128)(2,1)S(1)} %get-tuple-element.137), kind=kOutput, calls=%fused_computation.21 | convolution fusion | flops 1890975744 | bytes 10616832 | tf_op jit(solution)/shard_map/dot_general | solution.py:251
  114.6 4.3 fusion.11
  124.5 4.4 multiply_reduce_fusion.3
  168.5 5.2 reshape.1210
  179.5 4.3 gather_fusion.8
  183.8 4.0 multiply_reduce_fusion.4
  192.0 4.6 convert_bitcast_fusion.4
  203.6 4.2 gather_fusion.6
  213.1 4.3 fusion.17
  224.4 5.8 reshape.1201
  233.5 4.1 gather_fusion.4
  237.6 5.2 reshape.1196
  246.3 4.1 gather_fusion.2
  252.3 5.3 broadcast_select_fusion
  266.9 7.6 collective-permute-done.103
  277.3 11.4 %collective-permute-done.123 = bf16[2,2,1,8,48,384]{5,4,3,2,1,0:T(8,128)(2,1)S(1)} collective-permute-done((bf16[2,2,1,8,48,384]{5,4,3,2,1,0:T(8,128)(2,1)S(1)}, bf16[2,2,1,8,48,384]{5,4,3,2,1,0:T(8,128)(2,1)S(1)}, u32[]{:S(2)}, u32[]{:S(2)}) %collective-permute-start.123) | collective-permute-done | bytes 1179680 | tf_op jit(solution)/shard_map/ppermute | solution.py:99
  299.2 4.2 fusion.62
  348.0 4.3 collective-permute-start.112
  365.5 4.1 collective-permute-start.72
  380.6 4.1 collective-permute-start.132
  396.7 4.2 collective-permute-start.52
  411.9 4.1 collective-permute-start.92
  419.5 4.1 collective-permute-start.118
  438.3 4.1 collective-permute-start.119
  446.8 5.0 collective-permute-start.75
  453.1 4.5 collective-permute-done.73
  457.7 5.5 collective-permute-done.74
  463.8 4.1 collective-permute-start.138
  483.8 4.2 collective-permute-start.139
  492.4 4.8 collective-permute-start.55
  498.4 4.6 collective-permute-done.53
  503.0 5.2 collective-permute-done.54
  508.7 4.1 collective-permute-start.98
  527.8 4.2 collective-permute-start.99
  532.1 24.3 %collective-permute-start.80 = (bf16[1,1,1,8,48,384]{5,4,3,2,1,0:T(8,128)(2,1)S(1)}, bf16[1,1,1,8,48,384]{5,4,3,2,1,0:T(8,128)(2,1)S(1)}, u32[]{:S(2)}, u32[]{:S(2)}) collective-permute-start(bf16[1,1,1,8,48,384]{5,4,3,2,1,0:T(8,128)(2,1)S(1)} %bitcast.558), channel_id=1, source_target_pairs={{0,32},{1,97},{2,34},{3,99},{4,36},{5,101},{6,38},{7,103},{8,40},{... | collective-permute-start | bytes 884744 | tf_op jit(solution)/shard_map/ppermute | solution.py:99
  558.8 4.3 collective-permute-start.121
  575.0 4.5 collective-permute-done.141
  618.9 9.4 %broadcast_select_fusion.1 = (bf16[64,48,384]{2,1,0:T(8,128)(2,1)}, bf16[64,48,384]{2,1,0:T(8,128)(2,1)S(1)}, bf16[64,48,384]{2,1,0:T(8,128)(2,1)}, bf16[64,48,3...) fusion(bf16[64,48,384]{2,1,0:T(8,128)(2,1)} %gather_fusion.11, ...), kind=kLoop, calls=%fused_computation.101 | loop fusion | flops 7077888 | bytes 28311616 | tf_op jit(solution)/shard_map/jit(_take)/select_n | solution.py:136
  628.9 16.0 %collective-permute-done.16 = bf16[1,2,2,8,48,384]{5,4,3,2,1,0:T(8,128)(2,1)S(1)} collective-permute-done((bf16[1,2,2,8,48,384]{5,4,3,2,1,0:T(8,128)(2,1)S(1)}, bf16[1,2,2,8,48,384]{5,4,3,2,1,0:T(8,128)(2,1)S(1)}, u32[]{:S(2)}, u32[]{:S(2)}) %collective-permute-start.16) | collective-permute-done | bytes 1179680 | tf_op jit(solution)/shard_map/ppermute | solution.py:99
  646.1 8.9 %collective-permute-done.17 = bf16[1,2,1,8,48,384]{5,4,3,2,1,0:T(8,128)(2,1)S(1)} collective-permute-done((bf16[1,2,1,8,48,384]{5,4,3,2,1,0:T(8,128)(2,1)S(1)}, bf16[1,2,1,8,48,384]{5,4,3,2,1,0:T(8,128)(2,1)S(1)}, u32[]{:S(2)}, u32[]{:S(2)}) %collective-permute-start.17) | collective-permute-done | bytes 589856 | tf_op jit(solution)/shard_map/ppermute | solution.py:99
  676.9 4.1 collective-permute-done.40
  727.2 5.2 collective-permute-done.28
  735.8 4.7 collective-permute-done.32
  742.0 5.4 collective-permute-done.33
  750.5 7.0 collective-permute-done.34
  758.6 8.1 %collective-permute-start.35 = (bf16[1,2,2,8,48,384]{5,4,3,2,1,0:T(8,128)(2,1)}, bf16[1,2,2,8,48,384]{5,4,3,2,1,0:T(8,128)(2,1)}, u32[]{:S(2)}, u32[]{:S(2)}) collective-permute-start(bf16[1,2,2,8,48,384]{5,4,3,2,1,0:T(8,128)(2,1)} %pad_maximum_fusion.14), channel_id=1, source_target_pairs={{0,32},{1,97},{2,34},{3,99},{4,36},{5,101},{6,38},{7,103},{8,40},{... | collective-permute-start | bytes 3538952 | tf_op jit(solution)/shard_map/ppermute | solution.py:99
  (936 shorter events, 505.9 us)
Async XLA Ops:
  157.6 26.3 %collective-permute-start.11 = (bf16[384,768]{1,0:T(8,128)(2,1)}, bf16[384,768]{1,0:T(8,128)(2,1)}, u32[]{:S(2)}, u32[]{:S(2)}) collective-permute-start(bf16[384,768]{1,0:T(8,128)(2,1)} %dynamic-slice_convert_fusion.2), channel_id=1, source_target_pairs={{0,1},{1,0},{2,3},{3,2},{4,5},{5,4},{6,7},{7,6},{8,9},{9,8},{10,11... | collective-permute-start | bytes 1769480 | tf_op jit(solution)/shard_map/ppermute | solution.py:71
  188.5 19.3 %collective-permute-start.12 = (bf16[384,768]{1,0:T(8,128)(2,1)S(1)}, bf16[384,768]{1,0:T(8,128)(2,1)}, u32[]{:S(2)}, u32[]{:S(2)}) collective-permute-start(bf16[384,768]{1,0:T(8,128)(2,1)S(1)} %fusion.189), channel_id=1, source_target_pairs={{0,1},{1,0},{2,3},{3,2},{4,5},{5,4},{6,7},{7,6},{8,9},{9,8},{10,11... | collective-permute-start | bytes 1769480 | tf_op jit(solution)/shard_map/ppermute | solution.py:55
  261.2 27.4 %collective-permute-start.123 = (bf16[2,2,1,8,48,384]{5,4,3,2,1,0:T(8,128)(2,1)S(1)}, bf16[2,2,1,8,48,384]{5,4,3,2,1,0:T(8,128)(2,1)S(1)}, u32[]{:S(2)}, u32[]{:S(2)}) collective-permute-start(bf16[2,2,1,8,48,384]{5,4,3,2,1,0:T(8,128)(2,1)S(1)} %slice.1649), channel_id=1, source_target_pairs={{0,2},{1,7},{2,0},{3,5},{4,6},{5,3},{6,4},{7,1},{8,10},{9,15},{10,... | collective-permute-start | bytes 3538952 | tf_op jit(solution)/shard_map/ppermute | solution.py:99
  261.8 28.2 %collective-permute-start.43 = (bf16[2,1,2,8,48,384]{5,4,3,2,1,0:T(8,128)(2,1)S(1)}, bf16[2,1,2,8,48,384]{5,4,3,2,1,0:T(8,128)(2,1)S(1)}, u32[]{:S(2)}, u32[]{:S(2)}) collective-permute-start(bf16[2,1,2,8,48,384]{5,4,3,2,1,0:T(8,128)(2,1)S(1)} %slice.1490), channel_id=1, source_target_pairs={{0,8},{1,25},{2,10},{3,27},{4,12},{5,29},{6,14},{7,31},{8,0},{9,17... | collective-permute-start | bytes 3538952 | tf_op jit(solution)/shard_map/ppermute | solution.py:99
  262.6 30.1 %collective-permute-start.83 = (bf16[1,2,2,8,48,384]{5,4,3,2,1,0:T(8,128)(2,1)S(1)}, bf16[1,2,2,8,48,384]{5,4,3,2,1,0:T(8,128)(2,1)S(1)}, u32[]{:S(2)}, u32[]{:S(2)}) collective-permute-start(bf16[1,2,2,8,48,384]{5,4,3,2,1,0:T(8,128)(2,1)S(1)} %bitcast.580), channel_id=1, source_target_pairs={{0,32},{1,97},{2,34},{3,99},{4,36},{5,101},{6,38},{7,103},{8,40},{... | collective-permute-start | bytes 3538952 | tf_op jit(solution)/shard_map/ppermute | solution.py:99
  274.5 19.5 %collective-permute-start.14 = (bf16[384,768]{1,0:T(8,128)(2,1)S(1)}, bf16[384,768]{1,0:T(8,128)(2,1)S(1)}, u32[]{:S(2)}, u32[]{:S(2)}) collective-permute-start(bf16[384,768]{1,0:T(8,128)(2,1)S(1)} %get-tuple-element.59), channel_id=1, source_target_pairs={{0,1},{1,0},{2,3},{3,2},{4,5},{5,4},{6,7},{7,6},{8,9},{9,8},{10,11... | collective-permute-start | bytes 1769480 | tf_op jit(solution)/shard_map/ppermute | solution.py:55
  276.0 45.5 %collective-permute-start.104 = (bf16[1,1,2,8,48,384]{5,4,3,2,1,0:T(8,128)(2,1)}, bf16[1,1,2,8,48,384]{5,4,3,2,1,0:T(8,128)(2,1)}, u32[]{:S(2)}, u32[]{:S(2)}) collective-permute-start(bf16[1,1,2,8,48,384]{5,4,3,2,1,0:T(8,128)(2,1)} %add_convert_fusion.1), channel_id=1, source_target_pairs={{0,32},{1,97},{2,34},{3,99},{4,36},{5,101},{6,38},{7,103},{8,40},{... | collective-permute-start | bytes 1769480 | tf_op jit(solution)/shard_map/ppermute | solution.py:99
  288.7 35.0 %collective-permute-start.64 = (bf16[2,1,1,8,48,384]{5,4,3,2,1,0:T(8,128)(2,1)}, bf16[2,1,1,8,48,384]{5,4,3,2,1,0:T(8,128)(2,1)}, u32[]{:S(2)}, u32[]{:S(2)}) collective-permute-start(bf16[2,1,1,8,48,384]{5,4,3,2,1,0:T(8,128)(2,1)} %add_convert_fusion.3), channel_id=1, source_target_pairs={{0,8},{1,25},{2,10},{3,27},{4,12},{5,29},{6,14},{7,31},{8,0},{9,17... | collective-permute-start | bytes 1769480 | tf_op jit(solution)/shard_map/ppermute | solution.py:99
  290.1 36.7 %collective-permute-start.124 = (bf16[2,1,1,8,48,384]{5,4,3,2,1,0:T(8,128)(2,1)}, bf16[2,1,1,8,48,384]{5,4,3,2,1,0:T(8,128)(2,1)}, u32[]{:S(2)}, u32[]{:S(2)}) collective-permute-start(bf16[2,1,1,8,48,384]{5,4,3,2,1,0:T(8,128)(2,1)} %add_convert_fusion), channel_id=1, source_target_pairs={{0,8},{1,25},{2,10},{3,27},{4,12},{5,29},{6,14},{7,31},{8,0},{9,17... | collective-permute-start | bytes 1769480 | tf_op jit(solution)/shard_map/ppermute | solution.py:99
  292.7 35.4 %collective-permute-start.44 = (bf16[1,1,2,8,48,384]{5,4,3,2,1,0:T(8,128)(2,1)}, bf16[1,1,2,8,48,384]{5,4,3,2,1,0:T(8,128)(2,1)}, u32[]{:S(2)}, u32[]{:S(2)}) collective-permute-start(bf16[1,1,2,8,48,384]{5,4,3,2,1,0:T(8,128)(2,1)} %add_convert_fusion.4), channel_id=1, source_target_pairs={{0,32},{1,97},{2,34},{3,99},{4,36},{5,101},{6,38},{7,103},{8,40},{... | collective-permute-start | bytes 1769480 | tf_op jit(solution)/shard_map/ppermute | solution.py:99
  293.9 36.9 %collective-permute-start.84 = (bf16[1,2,1,8,48,384]{5,4,3,2,1,0:T(8,128)(2,1)}, bf16[1,2,1,8,48,384]{5,4,3,2,1,0:T(8,128)(2,1)}, u32[]{:S(2)}, u32[]{:S(2)}) collective-permute-start(bf16[1,2,1,8,48,384]{5,4,3,2,1,0:T(8,128)(2,1)} %add_convert_fusion.2), channel_id=1, source_target_pairs={{0,2},{1,7},{2,0},{3,5},{4,6},{5,3},{6,4},{7,1},{8,10},{9,15},{10,... | collective-permute-start | bytes 1769480 | tf_op jit(solution)/shard_map/ppermute | solution.py:99
  329.4 16.5 %collective-permute-start.45 = (bf16[1,1,1,8,48,384]{5,4,3,2,1,0:T(8,128)(2,1)S(1)}, bf16[1,1,1,8,48,384]{5,4,3,2,1,0:T(8,128)(2,1)S(1)}, u32[]{:S(2)}, u32[]{:S(2)}) collective-permute-start(bf16[1,1,1,8,48,384]{5,4,3,2,1,0:T(8,128)(2,1)S(1)} %add_convert_fusion.10), channel_id=1, source_target_pairs={{0,2},{1,7},{2,0},{3,5},{4,6},{5,3},{6,4},{7,1},{8,10},{9,15},{10,... | collective-permute-start | bytes 884744 | tf_op jit(solution)/shard_map/ppermute | solution.py:99
  333.4 20.7 %collective-permute-start.107 = (bf16[48,384]{1,0:T(8,128)(2,1)S(1)}, bf16[48,384]{1,0:T(8,128)(2,1)S(1)}, u32[]{:S(2)}, u32[]{:S(2)}) collective-permute-start(bf16[48,384]{1,0:T(8,128)(2,1)S(1)} %get-tuple-element.85), channel_id=1, source_target_pairs={{0,24},{1,9},{2,26},{3,11},{4,28},{5,13},{6,30},{7,15},{8,16},{9,1... | collective-permute-start | bytes 110600 | tf_op jit(solution)/shard_map/ppermute | solution.py:99
  337.6 18.3 %collective-permute-start.109 = (bf16[48,384]{1,0:T(8,128)(2,1)S(1)}, bf16[48,384]{1,0:T(8,128)(2,1)S(1)}, u32[]{:S(2)}, u32[]{:S(2)}) collective-permute-start(bf16[48,384]{1,0:T(8,128)(2,1)S(1)} %get-tuple-element.86), channel_id=1, source_target_pairs={{0,96},{1,33},{2,98},{3,35},{4,100},{5,37},{6,102},{7,39},{8,104},... | collective-permute-start | bytes 110600 | tf_op jit(solution)/shard_map/ppermute | solution.py:99
  419.5 27.4 %collective-permute-start.118 = (bf16[48,384]{1,0:T(8,128)(2,1)S(1)}, bf16[48,384]{1,0:T(8,128)(2,1)S(1)}, u32[]{:S(2)}, u32[]{:S(2)}) collective-permute-start(bf16[48,384]{1,0:T(8,128)(2,1)S(1)} %get-tuple-element.48), channel_id=1, source_target_pairs={{0,120},{1,41},{2,122},{3,43},{4,124},{5,45},{6,126},{7,47},{8,112... | collective-permute-start | bytes 110600 | tf_op jit(solution)/shard_map/ppermute | solution.py:99
  423.6 21.6 %collective-permute-start.117 = (bf16[48,384]{1,0:T(8,128)(2,1)S(1)}, bf16[48,384]{1,0:T(8,128)(2,1)S(1)}, u32[]{:S(2)}, u32[]{:S(2)}) collective-permute-start(bf16[48,384]{1,0:T(8,128)(2,1)S(1)} %get-tuple-element.48), channel_id=1, source_target_pairs={{0,102},{1,35},{2,100},{3,33},{4,98},{5,39},{6,96},{7,37},{8,110},... | collective-permute-start | bytes 110600 | tf_op jit(solution)/shard_map/ppermute | solution.py:99
  425.2 18.8 %collective-permute-start.116 = (bf16[48,384]{1,0:T(8,128)(2,1)S(1)}, bf16[48,384]{1,0:T(8,128)(2,1)S(1)}, u32[]{:S(2)}, u32[]{:S(2)}) collective-permute-start(bf16[48,384]{1,0:T(8,128)(2,1)S(1)} %get-tuple-element.48), channel_id=1, source_target_pairs={{0,96},{1,33},{2,98},{3,35},{4,100},{5,37},{6,102},{7,39},{8,104},... | collective-permute-start | bytes 110600 | tf_op jit(solution)/shard_map/ppermute | solution.py:99
  442.4 29.4 %collective-permute-start.78 = (bf16[48,384]{1,0:T(8,128)(2,1)S(1)}, bf16[48,384]{1,0:T(8,128)(2,1)S(1)}, u32[]{:S(2)}, u32[]{:S(2)}) collective-permute-start(bf16[48,384]{1,0:T(8,128)(2,1)S(1)} %get-tuple-element.52), channel_id=1, source_target_pairs={{0,120},{1,41},{2,122},{3,43},{4,124},{5,45},{6,126},{7,47},{8,112... | collective-permute-start | bytes 110600 | tf_op jit(solution)/shard_map/ppermute | solution.py:99
  444.1 25.6 %collective-permute-start.77 = (bf16[48,384]{1,0:T(8,128)(2,1)S(1)}, bf16[48,384]{1,0:T(8,128)(2,1)S(1)}, u32[]{:S(2)}, u32[]{:S(2)}) collective-permute-start(bf16[48,384]{1,0:T(8,128)(2,1)S(1)} %get-tuple-element.52), channel_id=1, source_target_pairs={{0,102},{1,35},{2,100},{3,33},{4,98},{5,39},{6,96},{7,37},{8,110},... | collective-permute-start | bytes 110600 | tf_op jit(solution)/shard_map/ppermute | solution.py:99
  445.2 22.8 %collective-permute-start.76 = (bf16[48,384]{1,0:T(8,128)(2,1)S(1)}, bf16[48,384]{1,0:T(8,128)(2,1)S(1)}, u32[]{:S(2)}, u32[]{:S(2)}) collective-permute-start(bf16[48,384]{1,0:T(8,128)(2,1)S(1)} %get-tuple-element.52), channel_id=1, source_target_pairs={{0,96},{1,33},{2,98},{3,35},{4,100},{5,37},{6,102},{7,39},{8,104},... | collective-permute-start | bytes 110600 | tf_op jit(solution)/shard_map/ppermute | solution.py:99
  446.8 17.0 %collective-permute-start.75 = (bf16[48,384]{1,0:T(8,128)(2,1)S(1)}, bf16[48,384]{1,0:T(8,128)(2,1)S(1)}, u32[]{:S(2)}, u32[]{:S(2)}) collective-permute-start(bf16[48,384]{1,0:T(8,128)(2,1)S(1)} %get-tuple-element.52), channel_id=1, source_target_pairs={{0,30},{1,11},{2,28},{3,9},{4,26},{5,15},{6,24},{7,13},{8,22},{9,3... | collective-permute-start | bytes 110600 | tf_op jit(solution)/shard_map/ppermute | solution.py:99
  463.8 28.5 %collective-permute-start.138 = (bf16[48,384]{1,0:T(8,128)(2,1)S(1)}, bf16[48,384]{1,0:T(8,128)(2,1)S(1)}, u32[]{:S(2)}, u32[]{:S(2)}) collective-permute-start(bf16[48,384]{1,0:T(8,128)(2,1)S(1)} %get-tuple-element.46), channel_id=1, source_target_pairs={{0,120},{1,41},{2,122},{3,43},{4,124},{5,45},{6,126},{7,47},{8,112... | collective-permute-start | bytes 110600 | tf_op jit(solution)/shard_map/ppermute | solution.py:99
  468.0 22.9 %collective-permute-start.137 = (bf16[48,384]{1,0:T(8,128)(2,1)S(1)}, bf16[48,384]{1,0:T(8,128)(2,1)S(1)}, u32[]{:S(2)}, u32[]{:S(2)}) collective-permute-start(bf16[48,384]{1,0:T(8,128)(2,1)S(1)} %get-tuple-element.46), channel_id=1, source_target_pairs={{0,102},{1,35},{2,100},{3,33},{4,98},{5,39},{6,96},{7,37},{8,110},... | collective-permute-start | bytes 110600 | tf_op jit(solution)/shard_map/ppermute | solution.py:99
  469.6 20.0 %collective-permute-start.136 = (bf16[48,384]{1,0:T(8,128)(2,1)S(1)}, bf16[48,384]{1,0:T(8,128)(2,1)S(1)}, u32[]{:S(2)}, u32[]{:S(2)}) collective-permute-start(bf16[48,384]{1,0:T(8,128)(2,1)S(1)} %get-tuple-element.46), channel_id=1, source_target_pairs={{0,96},{1,33},{2,98},{3,35},{4,100},{5,37},{6,102},{7,39},{8,104},... | collective-permute-start | bytes 110600 | tf_op jit(solution)/shard_map/ppermute | solution.py:99
  488.0 28.6 %collective-permute-start.58 = (bf16[48,384]{1,0:T(8,128)(2,1)S(1)}, bf16[48,384]{1,0:T(8,128)(2,1)S(1)}, u32[]{:S(2)}, u32[]{:S(2)}) collective-permute-start(bf16[48,384]{1,0:T(8,128)(2,1)S(1)} %get-tuple-element.54), channel_id=1, source_target_pairs={{0,120},{1,41},{2,122},{3,43},{4,124},{5,45},{6,126},{7,47},{8,112... | collective-permute-start | bytes 110600 | tf_op jit(solution)/shard_map/ppermute | solution.py:99
  489.6 25.0 %collective-permute-start.57 = (bf16[48,384]{1,0:T(8,128)(2,1)S(1)}, bf16[48,384]{1,0:T(8,128)(2,1)S(1)}, u32[]{:S(2)}, u32[]{:S(2)}) collective-permute-start(bf16[48,384]{1,0:T(8,128)(2,1)S(1)} %get-tuple-element.54), channel_id=1, source_target_pairs={{0,102},{1,35},{2,100},{3,33},{4,98},{5,39},{6,96},{7,37},{8,110},... | collective-permute-start | bytes 110600 | tf_op jit(solution)/shard_map/ppermute | solution.py:99
  490.8 22.0 %collective-permute-start.56 = (bf16[48,384]{1,0:T(8,128)(2,1)S(1)}, bf16[48,384]{1,0:T(8,128)(2,1)S(1)}, u32[]{:S(2)}, u32[]{:S(2)}) collective-permute-start(bf16[48,384]{1,0:T(8,128)(2,1)S(1)} %get-tuple-element.54), channel_id=1, source_target_pairs={{0,96},{1,33},{2,98},{3,35},{4,100},{5,37},{6,102},{7,39},{8,104},... | collective-permute-start | bytes 110600 | tf_op jit(solution)/shard_map/ppermute | solution.py:99
  492.4 16.3 %collective-permute-start.55 = (bf16[48,384]{1,0:T(8,128)(2,1)S(1)}, bf16[48,384]{1,0:T(8,128)(2,1)S(1)}, u32[]{:S(2)}, u32[]{:S(2)}) collective-permute-start(bf16[48,384]{1,0:T(8,128)(2,1)S(1)} %get-tuple-element.54), channel_id=1, source_target_pairs={{0,30},{1,11},{2,28},{3,9},{4,26},{5,15},{6,24},{7,13},{8,22},{9,3... | collective-permute-start | bytes 110600 | tf_op jit(solution)/shard_map/ppermute | solution.py:99
  508.7 47.8 %collective-permute-start.98 = (bf16[48,384]{1,0:T(8,128)(2,1)S(1)}, bf16[48,384]{1,0:T(8,128)(2,1)S(1)}, u32[]{:S(2)}, u32[]{:S(2)}) collective-permute-start(bf16[48,384]{1,0:T(8,128)(2,1)S(1)} %get-tuple-element.50), channel_id=1, source_target_pairs={{0,120},{1,41},{2,122},{3,43},{4,124},{5,45},{6,126},{7,47},{8,112... | collective-permute-start | bytes 110600 | tf_op jit(solution)/shard_map/ppermute | solution.py:99
  512.9 43.6 %collective-permute-start.97 = (bf16[48,384]{1,0:T(8,128)(2,1)S(1)}, bf16[48,384]{1,0:T(8,128)(2,1)S(1)}, u32[]{:S(2)}, u32[]{:S(2)}) collective-permute-start(bf16[48,384]{1,0:T(8,128)(2,1)S(1)} %get-tuple-element.50), channel_id=1, source_target_pairs={{0,102},{1,35},{2,100},{3,33},{4,98},{5,39},{6,96},{7,37},{8,110},... | collective-permute-start | bytes 110600 | tf_op jit(solution)/shard_map/ppermute | solution.py:99
  514.6 17.5 %collective-permute-start.96 = (bf16[48,384]{1,0:T(8,128)(2,1)S(1)}, bf16[48,384]{1,0:T(8,128)(2,1)S(1)}, u32[]{:S(2)}, u32[]{:S(2)}) collective-permute-start(bf16[48,384]{1,0:T(8,128)(2,1)S(1)} %get-tuple-element.50), channel_id=1, source_target_pairs={{0,96},{1,33},{2,98},{3,35},{4,100},{5,37},{6,102},{7,39},{8,104},... | collective-permute-start | bytes 110600 | tf_op jit(solution)/shard_map/ppermute | solution.py:99
  527.8 30.8 %collective-permute-start.99 = (bf16[48,384]{1,0:T(8,128)(2,1)S(1)}, bf16[48,384]{1,0:T(8,128)(2,1)S(1)}, u32[]{:S(2)}, u32[]{:S(2)}) collective-permute-start(bf16[48,384]{1,0:T(8,128)(2,1)S(1)} %get-tuple-element.50), channel_id=1, source_target_pairs={{0,126},{1,43},{2,124},{3,41},{4,122},{5,47},{6,120},{7,45},{8,118... | collective-permute-start | bytes 110600 | tf_op jit(solution)/shard_map/ppermute | solution.py:99
  532.0 26.7 %collective-permute-start.120 = (bf16[1,1,1,8,48,384]{5,4,3,2,1,0:T(8,128)(2,1)S(1)}, bf16[1,1,1,8,48,384]{5,4,3,2,1,0:T(8,128)(2,1)S(1)}, u32[]{:S(2)}, u32[]{:S(2)}) collective-permute-start(bf16[1,1,1,8,48,384]{5,4,3,2,1,0:T(8,128)(2,1)S(1)} %bitcast.562), channel_id=1, source_target_pairs={{0,2},{1,7},{2,0},{3,5},{4,6},{5,3},{6,4},{7,1},{8,10},{9,15},{10,... | collective-permute-start | bytes 884744 | tf_op jit(solution)/shard_map/ppermute | solution.py:99
  532.1 31.0 %collective-permute-start.80 = (bf16[1,1,1,8,48,384]{5,4,3,2,1,0:T(8,128)(2,1)S(1)}, bf16[1,1,1,8,48,384]{5,4,3,2,1,0:T(8,128)(2,1)S(1)}, u32[]{:S(2)}, u32[]{:S(2)}) collective-permute-start(bf16[1,1,1,8,48,384]{5,4,3,2,1,0:T(8,128)(2,1)S(1)} %bitcast.558), channel_id=1, source_target_pairs={{0,32},{1,97},{2,34},{3,99},{4,36},{5,101},{6,38},{7,103},{8,40},{... | collective-permute-start | bytes 884744 | tf_op jit(solution)/shard_map/ppermute | solution.py:99
  565.7 18.1 %collective-permute-start.61 = (bf16[1,1,2,8,48,384]{5,4,3,2,1,0:T(8,128)(2,1)S(1)}, bf16[1,1,2,8,48,384]{5,4,3,2,1,0:T(8,128)(2,1)S(1)}, u32[]{:S(2)}, u32[]{:S(2)}) collective-permute-start(bf16[1,1,2,8,48,384]{5,4,3,2,1,0:T(8,128)(2,1)S(1)} %pad_maximum_fusion.33), channel_id=1, source_target_pairs={{0,32},{1,97},{2,34},{3,99},{4,36},{5,101},{6,38},{7,103},{8,40},{... | collective-permute-start | bytes 1769480 | tf_op jit(solution)/shard_map/ppermute | solution.py:99
  566.8 18.3 %collective-permute-start.101 = (bf16[1,2,1,8,48,384]{5,4,3,2,1,0:T(8,128)(2,1)S(1)}, bf16[1,2,1,8,48,384]{5,4,3,2,1,0:T(8,128)(2,1)S(1)}, u32[]{:S(2)}, u32[]{:S(2)}) collective-permute-start(bf16[1,2,1,8,48,384]{5,4,3,2,1,0:T(8,128)(2,1)S(1)} %pad_maximum_fusion.35), channel_id=1, source_target_pairs={{0,2},{1,7},{2,0},{3,5},{4,6},{5,3},{6,4},{7,1},{8,10},{9,15},{10,... | collective-permute-start | bytes 1769480 | tf_op jit(solution)/shard_map/ppermute | solution.py:99
  572.2 25.7 %collective-permute-start.122 = (bf16[2,1,2,8,48,384]{5,4,3,2,1,0:T(8,128)(2,1)}, bf16[2,1,2,8,48,384]{5,4,3,2,1,0:T(8,128)(2,1)}, u32[]{:S(2)}, u32[]{:S(2)}) collective-permute-start(bf16[2,1,2,8,48,384]{5,4,3,2,1,0:T(8,128)(2,1)} %pad_maximum_fusion.18), channel_id=1, source_target_pairs={{0,8},{1,25},{2,10},{3,27},{4,12},{5,29},{6,14},{7,31},{8,0},{9,17... | collective-permute-start | bytes 3538952 | tf_op jit(solution)/shard_map/ppermute | solution.py:99
  574.4 27.7 %collective-permute-start.82 = (bf16[2,2,1,8,48,384]{5,4,3,2,1,0:T(8,128)(2,1)}, bf16[2,2,1,8,48,384]{5,4,3,2,1,0:T(8,128)(2,1)}, u32[]{:S(2)}, u32[]{:S(2)}) collective-permute-start(bf16[2,2,1,8,48,384]{5,4,3,2,1,0:T(8,128)(2,1)} %pad_maximum_fusion.16), channel_id=1, source_target_pairs={{0,2},{1,7},{2,0},{3,5},{4,6},{5,3},{6,4},{7,1},{8,10},{9,15},{10,... | collective-permute-start | bytes 3538952 | tf_op jit(solution)/shard_map/ppermute | solution.py:99
  580.7 25.6 %collective-permute-start.142 = (bf16[2,2,1,8,48,384]{5,4,3,2,1,0:T(8,128)(2,1)}, bf16[2,2,1,8,48,384]{5,4,3,2,1,0:T(8,128)(2,1)}, u32[]{:S(2)}, u32[]{:S(2)}) collective-permute-start(bf16[2,2,1,8,48,384]{5,4,3,2,1,0:T(8,128)(2,1)} %pad_maximum_fusion.19), channel_id=1, source_target_pairs={{0,2},{1,7},{2,0},{3,5},{4,6},{5,3},{6,4},{7,1},{8,10},{9,15},{10,... | collective-permute-start | bytes 3538952 | tf_op jit(solution)/shard_map/ppermute | solution.py:99
  585.0 25.4 %collective-permute-start.62 = (bf16[2,1,2,8,48,384]{5,4,3,2,1,0:T(8,128)(2,1)}, bf16[2,1,2,8,48,384]{5,4,3,2,1,0:T(8,128)(2,1)}, u32[]{:S(2)}, u32[]{:S(2)}) collective-permute-start(bf16[2,1,2,8,48,384]{5,4,3,2,1,0:T(8,128)(2,1)} %pad_maximum_fusion.15), channel_id=1, source_target_pairs={{0,8},{1,25},{2,10},{3,27},{4,12},{5,29},{6,14},{7,31},{8,0},{9,17... | collective-permute-start | bytes 3538952 | tf_op jit(solution)/shard_map/ppermute | solution.py:99
  586.3 28.3 %collective-permute-start.102 = (bf16[1,2,2,8,48,384]{5,4,3,2,1,0:T(8,128)(2,1)}, bf16[1,2,2,8,48,384]{5,4,3,2,1,0:T(8,128)(2,1)}, u32[]{:S(2)}, u32[]{:S(2)}) collective-permute-start(bf16[1,2,2,8,48,384]{5,4,3,2,1,0:T(8,128)(2,1)} %pad_maximum_fusion.17), channel_id=1, source_target_pairs={{0,32},{1,97},{2,34},{3,99},{4,36},{5,101},{6,38},{7,103},{8,40},{... | collective-permute-start | bytes 3538952 | tf_op jit(solution)/shard_map/ppermute | solution.py:99
  656.0 34.8 %collective-permute-start.18 = (bf16[1,1,1,8,48,384]{5,4,3,2,1,0:T(8,128)(2,1)}, bf16[1,1,1,8,48,384]{5,4,3,2,1,0:T(8,128)(2,1)}, u32[]{:S(2)}, u32[]{:S(2)}) collective-permute-start(bf16[1,1,1,8,48,384]{5,4,3,2,1,0:T(8,128)(2,1)} %add_convert_fusion.11), channel_id=1, source_target_pairs={{0,8},{1,25},{2,10},{3,27},{4,12},{5,29},{6,14},{7,31},{8,0},{9,17... | collective-permute-start | bytes 884744 | tf_op jit(solution)/shard_map/ppermute | solution.py:99
  694.0 16.9 %collective-permute-start.21 = (bf16[48,384]{1,0:T(8,128)(2,1)S(1)}, bf16[48,384]{1,0:T(8,128)(2,1)S(1)}, u32[]{:S(2)}, u32[]{:S(2)}) collective-permute-start(bf16[48,384]{1,0:T(8,128)(2,1)S(1)} %get-tuple-element.116), channel_id=1, source_target_pairs={{0,30},{1,11},{2,28},{3,9},{4,26},{5,15},{6,24},{7,13},{8,22},{9,3... | collective-permute-start | bytes 110600 | tf_op jit(solution)/shard_map/ppermute | solution.py:99
  714.9 25.8 %collective-permute-start.15 = (bf16[384,768]{1,0:T(8,128)(2,1)S(1)}, bf16[384,768]{1,0:T(8,128)(2,1)S(1)}, u32[]{:S(2)}, u32[]{:S(2)}) collective-permute-start(bf16[384,768]{1,0:T(8,128)(2,1)S(1)} %dynamic-slice_convert_fusion), channel_id=1, source_target_pairs={{0,1},{1,0},{2,3},{3,2},{4,5},{5,4},{6,7},{7,6},{8,9},{9,8},{10,11... | collective-permute-start | bytes 1769480 | tf_op jit(solution)/shard_map/ppermute | solution.py:71
  714.9 20.9 %collective-permute-start.31 = (bf16[48,384]{1,0:T(8,128)(2,1)S(1)}, bf16[48,384]{1,0:T(8,128)(2,1)S(1)}, u32[]{:S(2)}, u32[]{:S(2)}) collective-permute-start(bf16[48,384]{1,0:T(8,128)(2,1)S(1)} %get-tuple-element.56), channel_id=1, source_target_pairs={{0,120},{1,41},{2,122},{3,43},{4,124},{5,45},{6,126},{7,47},{8,112... | collective-permute-start | bytes 110600 | tf_op jit(solution)/shard_map/ppermute | solution.py:99
  716.5 19.3 %collective-permute-start.30 = (bf16[48,384]{1,0:T(8,128)(2,1)S(1)}, bf16[48,384]{1,0:T(8,128)(2,1)S(1)}, u32[]{:S(2)}, u32[]{:S(2)}) collective-permute-start(bf16[48,384]{1,0:T(8,128)(2,1)S(1)} %get-tuple-element.56), channel_id=1, source_target_pairs={{0,102},{1,35},{2,100},{3,33},{4,98},{5,39},{6,96},{7,37},{8,110},... | collective-permute-start | bytes 110600 | tf_op jit(solution)/shard_map/ppermute | solution.py:99
  718.3 17.4 %collective-permute-start.29 = (bf16[48,384]{1,0:T(8,128)(2,1)S(1)}, bf16[48,384]{1,0:T(8,128)(2,1)S(1)}, u32[]{:S(2)}, u32[]{:S(2)}) collective-permute-start(bf16[48,384]{1,0:T(8,128)(2,1)S(1)} %get-tuple-element.56), channel_id=1, source_target_pairs={{0,96},{1,33},{2,98},{3,35},{4,100},{5,37},{6,102},{7,39},{8,104},... | collective-permute-start | bytes 110600 | tf_op jit(solution)/shard_map/ppermute | solution.py:99
  758.6 32.1 %collective-permute-start.35 = (bf16[1,2,2,8,48,384]{5,4,3,2,1,0:T(8,128)(2,1)}, bf16[1,2,2,8,48,384]{5,4,3,2,1,0:T(8,128)(2,1)}, u32[]{:S(2)}, u32[]{:S(2)}) collective-permute-start(bf16[1,2,2,8,48,384]{5,4,3,2,1,0:T(8,128)(2,1)} %pad_maximum_fusion.14), channel_id=1, source_target_pairs={{0,32},{1,97},{2,34},{3,99},{4,36},{5,101},{6,38},{7,103},{8,40},{... | collective-permute-start | bytes 3538952 | tf_op jit(solution)/shard_map/ppermute | solution.py:99
  (288 other events, 2748.5 us)
